TPU v7x, 32 devices: a whole 2x2x4 slice. The times are simulated.
32 devices in a mesh: groups: 2 (over y), blk: 4 (over z), dp: 2 (over x), sub: 2 (over core).
Axes of the slice: x: 2, y: 2, z: 4, core: 2. Of those that a mesh axis runs over, the one named last changes fastest.
Arguments:
- view_a: bfloat16 [2048, 256], P(('groups', 'blk', 'dp', 'sub')), parts along dimension 0, may hold values from -6 to 6
- view_b: bfloat16 [2048, 256], P(('groups', 'blk', 'dp', 'sub')), parts along dimension 0, may hold values from -6 to 6
- prototypes: bfloat16 [32768, 256], P('blk'), may hold values from -6 to 6
- tile_mask: int32 [16, 256], replicated, may hold values from 0 to 1, as said below
- tile_region: int32 [32], P('groups'), parts along dimension 0, may hold values from 0 to 15, as said below
Outputs:
- grad_view_b: float32 [2048, 256], P(('groups', 'blk', 'dp', 'sub')), parts along dimension 0
- grad_prototypes: float32 [65536, 256], P(('groups', 'blk', 'dp', 'sub')), parts along dimension 0
There are 2 independent parts, one for each index of `groups`. A program takes and returns all parts, laid end to end along the dimension named above; an argument that names none is the same for every part. Nothing has to cross between parts.
Inputs may be any that keep to these rules, and one draw needn't show every extreme that they name: `tile_mask`: every prototype tile is 1 for at least one region, and every region for at least 16 tiles. `tile_region`: every region is named by at least one hit tile.
All inputs are finite; a program needn't handle non-finite values.
Results may differ from a plain program's by a relative error of at most 0.00045.
The roundings to bfloat16 on the way count: a program that leaves them out, or rounds other values in their place, can miss the bound.
Values may be sent and summed in bfloat16 or wider, within the bound.
A program may use at most 64 MiB of HBM per device.

v0:
```python
import jax
import jax.numpy as jnp
from jax import lax
from jax.sharding import PartitionSpec as P

TILE = 128
ITERS = 3
SOFTMAX_TEMPER = 0.1
EPSILON = 0.05
PART = ("blk", "dp", "sub")


def unit_rows(matrix):
    values = matrix.astype(jnp.float32)
    return (values * lax.rsqrt(jnp.sum(values * values, axis=1, keepdims=True) + 1e-06)).astype(
        jnp.bfloat16
    )


def body(view_a, view_b, prototypes, tile_mask, tile_region):
    n_dp = lax.axis_size("dp")
    n_sub = lax.axis_size("sub")
    blk_pos = lax.axis_index("blk")
    inner_pos = lax.axis_index("dp") * n_sub + lax.axis_index("sub")
    hit_dev, width = view_a.shape
    cols = prototypes.shape[0] // (n_dp * n_sub)
    tiles = cols // TILE
    regions = tile_mask.shape[0]
    protos = unit_rows(lax.dynamic_slice_in_dim(prototypes, inner_pos * cols, cols, 0))
    both = jnp.concatenate([unit_rows(view_a), unit_rows(view_b)], axis=1)
    both = lax.all_gather(both, PART, axis=0, tiled=True)
    rows_a, rows_b = (both[:, :width], both[:, width:])
    hits = rows_a.shape[0]
    own_tile = (blk_pos * n_dp * n_sub + inner_pos) * tiles
    my_mask = lax.dynamic_slice_in_dim(tile_mask, own_tile, tiles, 1).astype(jnp.float32)
    onehot = (tile_region[:, None] == jnp.arange(regions, dtype=jnp.int32)[None, :]).astype(
        jnp.float32
    )
    flags = jnp.dot(onehot, my_mask) > 0.5
    active = jnp.broadcast_to(
        flags[:, None, :, None], (hits // hit_dev, hit_dev, tiles, TILE)
    ).reshape(hits, cols)

    def scores(rows):
        return jnp.einsum("rd,kd->rk", rows, protos, preferred_element_type=jnp.float32)

    code_exp = jnp.where(active, jnp.exp((scores(rows_a) - 1.0) / EPSILON), 0.0).astype(
        jnp.bfloat16
    )
    pred = jnp.where(active, jnp.exp((scores(rows_b) - 1.0) / SOFTMAX_TEMPER), 0.0)
    norm = jnp.sum(pred, axis=1)
    code = code_exp.astype(jnp.float32)
    row = jnp.ones((hits,), jnp.float32)
    for sweep in range(ITERS):
        col = 1.0 / jnp.sum(code * row[:, None], axis=0)
        part = jnp.sum(code * col[None, :], axis=1)
        if sweep == 0:
            part, norm = lax.psum((part, norm), PART)
        else:
            part = lax.psum(part, PART)
        row = 1.0 / part
    grad = ((pred / norm[:, None] - row[:, None] * code * col[None, :]) / SOFTMAX_TEMPER).astype(
        jnp.bfloat16
    )
    hit_part = jnp.dot(grad, protos, preferred_element_type=jnp.float32)
    grad_protos = jnp.einsum("rk,rd->kd", grad, rows_b, preferred_element_type=jnp.float32)
    return (lax.psum_scatter(hit_part, PART, scatter_dimension=0, tiled=True), grad_protos)


def solution(mesh):
    spread = P(("groups", "blk", "dp", "sub"), None)
    return jax.shard_map(
        body,
        mesh=mesh,
        in_specs=(spread, spread, P("blk", None), P(), P("groups")),
        out_specs=(spread, spread),
        check_vma=False,
    )
```

profile of v0, /device:TPU:0, one launch (start us, length us, event | category | flops | bytes accessed | tf_op | source)
XLA Modules:
  0.0 244.8 jit_solution(6231227928295905269)
XLA Ops:
  7.2 0.0 all-gather.2.cloned.1.call-start
  7.2 0.9 fusion.17
  8.1 0.9 fusion.19
  9.0 0.9 fusion.18
  9.9 0.6 pad_maximum_fusion
  10.5 0.0 all-gather.2.cloned.1.call-update
  10.5 0.0 reduce-scatter.2.cloned.1.call-start
  10.6 1.6 fusion.10
  12.2 0.9 convolution_compare_fusion
  13.1 38.3 %all-gather.2.cloned.1.call-done = bf16[1024,512]{1,0:T(8,128)(2,1)} async-done(((bf16[64,512]{1,0:T(8,128)(2,1)}), bf16[1024,512]{1,0:T(8,128)(2,1)}) %all-gather.2.cloned.1.call-update) | async-done | bytes 1048592 | tf_op jit(solution)/shard_map/all_gather | solution.py:31
  51.4 0.6 broadcast_in_dim.6
  52.0 4.3 %convert_reduce_fusion = (f32[2048]{0:T(1024)S(1)}, bf16[1024,2048]{1,0:T(8,128)(2,1)S(1)}) fusion(f32[2048]{0:T(1024)S(1)} %add_rsqrt_fusion, bf16[8192,256]{1,0:T(8,128)(2,1)} %param.7, s32[]{:T(128)S(6)} %select_n.14, bf16[1024,512]{1,0:T(8,128)(2,1)} %all-gather.2.cloned.1.call-done, pred[128,8,16,128]{3,2,1,0:T(8,128)(4,1)S(1)} %bitcast.11), kind=kOutput, calls=%fused_computation.6 | convolution fusion | flops 1087895552 | bytes 7880708 | tf_op jit(solution)/shard_map/rd,kd->rk/dot_general | solution.py:45
  56.3 0.0 copy-start
  56.4 2.0 copy-done
  58.3 0.9 fusion
  59.2 31.6 %psum.29 = f32[1024]{0:T(1024)S(1)} all-reduce(f32[1024]{0:T(1024)S(1)} %fusion), channel_id=1, replica_groups=mesh['groups'=2,'blk'=4,'dp'=2,'sub'=2] {'blk','dp','sub'}, use_global_device_ids=true, to_apply=%region_7.8 | all-reduce | flops 1024 | bytes 8192 | tf_op jit(solution)/shard_map/psum | solution.py:58
  90.8 0.0 copy-start.2
  90.8 3.2 %fusion.1 = f32[2048]{0:T(1024)S(1)} fusion(bf16[1024,2048]{1,0:T(8,128)(2,1)} %copy-done, f32[1024]{0:T(1024)S(1)} %broadcast_divide_fusion.5), kind=kLoop, calls=%fused_computation.8 | loop fusion | flops 6289408 | bytes 4206592 | tf_op jit(solution)/shard_map/reduce_sum | solution.py:55
  94.0 3.1 %fusion.2 = f32[1024]{0:T(1024)S(1)} fusion(bf16[1024,2048]{1,0:T(8,128)(2,1)} %copy-done, f32[2048]{0:T(1024)S(1)} %broadcast_divide_fusion.1), kind=kLoop, calls=%fused_computation.9 | loop fusion | flops 6290432 | bytes 4206592 | tf_op jit(solution)/shard_map/reduce_sum | solution.py:56
  97.1 29.7 %psum.30 = f32[1024]{0:T(1024)S(1)} all-reduce(f32[1024]{0:T(1024)S(1)} %fusion.2), channel_id=1, replica_groups=mesh['groups'=2,'blk'=4,'dp'=2,'sub'=2] {'blk','dp','sub'}, use_global_device_ids=true, to_apply=%region_10.11 | all-reduce | flops 1024 | bytes 8192 | tf_op jit(solution)/shard_map/psum | solution.py:60
  126.8 3.1 %fusion.3 = f32[2048]{0:T(1024)S(1)} fusion(bf16[1024,2048]{1,0:T(8,128)(2,1)} %copy-done, f32[1024]{0:T(1024)S(1)} %broadcast_divide_fusion.4), kind=kLoop, calls=%fused_computation.10 | loop fusion | flops 6289408 | bytes 4206592 | tf_op jit(solution)/shard_map/reduce_sum | solution.py:55
  129.9 3.1 %fusion.4 = f32[1024]{0:T(1024)S(1)} fusion(bf16[1024,2048]{1,0:T(8,128)(2,1)} %copy-done, f32[2048]{0:T(1024)S(1)} %broadcast_divide_fusion), kind=kLoop, calls=%fused_computation.11 | loop fusion | flops 6290432 | bytes 4206592 | tf_op jit(solution)/shard_map/reduce_sum | solution.py:56
  132.9 0.0 copy-done.2
  132.9 7.3 %fusion.9 = (f32[1024]{0:T(1024)S(1)}, f32[1024,2048]{1,0:T(8,128)}) fusion(pred[128,8,16,128]{3,2,1,0:T(8,128)(4,1)S(1)} %bitcast.12, f32[2048]{0:T(1024)S(1)} %add_rsqrt_fusion, bf16[8192,256]{1,0:T(8,128)(2,1)} %param.7, s32[]{:T(128)S(6)} %select_n.14, bf16[1024,512]{1,0:T(8,128)(2,1)S(1)} %copy-done.2), kind=kOutput, calls=%fused_computation.18 | convolution fusion | flops 1083702272 | bytes 12070916 | tf_op jit(solution)/shard_map/rd,kd->rk/dot_general | solution.py:45
  140.2 30.0 %all-reduce = (f32[1024]{0:T(1024)S(1)}, f32[1024]{0:T(1024)S(1)}) all-reduce(f32[1024]{0:T(1024)S(1)} %fusion.4, f32[1024]{0:T(1024)S(1)} %get-tuple-element.6), channel_id=1, replica_groups=mesh['groups'=2,'blk'=4,'dp'=2,'sub'=2] {'blk','dp','sub'}, use_global_device_ids=true, to_apply=%region_13.14 | all-reduce | flops 2048 | bytes 16384 | tf_op jit(solution)/shard_map/psum | solution.py:60
  170.2 7.4 %fusion.8 = bf16[1024,2048]{1,0:T(8,128)(2,1)S(1)} fusion(bf16[1024,2048]{1,0:T(8,128)(2,1)} %copy-done, f32[1024,2048]{1,0:T(8,128)} %get-tuple-element.7, pred[128,8,16,128]{3,2,1,0:T(8,128)(4,1)S(1)} %bitcast.13, f32[1024]{0:T(1024)S(1)} %broadcast_divide_fusion.3, f32[2048]{0:T(1024)S(1)} %broadcast_divide_fusion, f32[1024]{0:T(1024)S(1)} %get-tuple-element.3), kind=kLoop, calls=%fused_computation.15 | loop fusion | flops 20971520 | bytes 18890752 | tf_op jit(solution)/shard_map/convert_element_type | solution.py:62
  177.6 0.0 copy-start.1
  177.7 1.9 copy-done.1
  179.6 3.6 %fusion.25 = f32[1024,256]{1,0:T(8,128)} fusion(bf16[1024,2048]{1,0:T(8,128)(2,1)S(1)} %fusion.8, f32[2048]{0:T(1024)S(1)} %add_rsqrt_fusion, bf16[8192,256]{1,0:T(8,128)(2,1)} %param.7, s32[]{:T(128)S(6)} %select_n.14), kind=kOutput, calls=%fused_computation.52 | convolution fusion | flops 1075314688 | bytes 6299652 | tf_op jit(solution)/shard_map/dot_general | solution.py:65
  183.1 0.0 reduce-scatter.2.cloned.1.call-update
  183.2 4.8 %fusion.13 = f32[2048,256]{1,0:T(8,128)} fusion(bf16[1024,2048]{1,0:T(8,128)(2,1)} %copy-done.1, bf16[1024,512]{1,0:T(8,128)(2,1)S(1)} %copy-done.2), kind=kOutput, calls=%fused_computation.25 | convolution fusion | flops 1073741824 | bytes 6815744 | tf_op jit(solution)/shard_map/rk,rd->kd/dot_general | solution.py:66
  188.0 49.9 %reduce-scatter.2.cloned.1.call-done = f32[64,256]{1,0:T(8,128)} async-done(((f32[1024,256]{1,0:T(8,128)}), f32[64,256]{1,0:T(8,128)}) %reduce-scatter.2.cloned.1.call-update) | async-done | bytes 65552 | tf_op jit(solution)/shard_map/reduce_scatter | solution.py:67
  (9 shorter events, 0.0 us)
Async XLA Ops:
  7.2 44.2 %all-gather.2.cloned.1.call-start = ((), (), s32[]{:S(2)}) async-start(), calls=%async_computation.1 | async-start | bytes 1114112 | tf_op jit(solution)/shard_map/all_gather | solution.py:31
  10.5 227.4 %reduce-scatter.2.cloned.1.call-start = ((), (), s32[]{:S(2)}) async-start(), calls=%async_computation.2 | async-start | bytes 1114112 | tf_op jit(solution)/shard_map/reduce_scatter | solution.py:67
  56.3 2.0 copy-start
  90.8 42.1 %copy-start.2 = (bf16[1024,512]{1,0:T(8,128)(2,1)S(1)}, bf16[1024,512]{1,0:T(8,128)(2,1)}, u32[]{:S(2)}) copy-start(bf16[1024,512]{1,0:T(8,128)(2,1)} %all-gather.2.cloned.1.call-done) | copy-start | bytes 3145732
  177.6 1.9 copy-start.1
Sparse Core Ops, SparseCore 0:
  10.7 40.6 all-gather.1
  183.3 54.6 reduce-scatter.1
where the time goes:
time: 245 us
  blocking collectives  91.2 us (37%)
  waiting for transfers between devices  88.3 us (36%)
  other arithmetic  25.6 us (10%)
  matrix products  20.9 us (9%)
  between operations  14.2 us (6%)
  local copies, waits for them, and re-layouts  4.48 us (2%)
    psum x2, blocking collectives, body(): part = lax.psum(part, PART)  59.6 us
    reduce_scatter x1, waiting for transfers between devices, body(): lax.psum_scatter(hit_part, PART, scatter_dimension=0, tiled=True)  49.9 us
    all_gather x1, waiting for transfers between devices, body(): both = lax.all_gather(both, PART, axis=0, tiled=True)  38.3 us
    psum x1, blocking collectives, body(): part, norm = lax.psum((part, norm), PART)  31.6 us
    dot_general x2, matrix products, scores(): jnp.einsum('rd,kd->rk', rows, protos, preferred_element_type=jnp.float32)  11.6 us
    convert_element_type x1, other arithmetic, body(): ((pred / norm[:, None] - row[:, None] * code * col[None, :]) / SOFTMAX_TE...  7.44 us
    reduce_sum x3, other arithmetic, body(): part = jnp.sum(code * col[None, :], axis=1)  7.06 us
    reduce_sum x2, other arithmetic, body(): col = 1.0 / jnp.sum(code * row[:, None], axis=0)  6.24 us
  transfers between devices with their start and end apart: 2, of which 2 were waited for; matrix products, arithmetic and copies ran while one was open for 3% of the time, Pallas kernels for 0%

commit v1 on v0

--- a/solution.py
+++ b/solution.py
@@ -55,7 +55,7 @@
         col = 1.0 / jnp.sum(code * row[:, None], axis=0)
         part = jnp.sum(code * col[None, :], axis=1)
         if sweep == 0:
-            part, norm = lax.psum((part, norm), PART)
+            part, norm = lax.psum(lax.psum((part, norm), ("dp", "sub")), "blk")
         else:
             part = lax.psum(part, PART)
         row = 1.0 / part

time: 245 us -> 229 us (0.935)
  blocking collectives: 91.2 us -> 76.1 us
    psum x1 -> x2, blocking collectives: 31.6 us -> 16.9 us  [body(): part, norm = lax.psum(lax.psum((part, norm), ('dp', 'sub')), 'blk')]
where the time goes in v1:
time: 229 us; the launch traced here: 228 us
  waiting for transfers between devices  88.3 us (39%)
  blocking collectives  76.1 us (33%)
  other arithmetic  25.5 us (11%)
  matrix products  21.5 us (9%)
  between operations  14.2 us (6%)
  local copies, waits for them, and re-layouts  2.53 us (1%)
    psum x2, blocking collectives, body(): part = lax.psum(part, PART)  59.2 us
    reduce_scatter x1, waiting for transfers between devices, body(): lax.psum_scatter(hit_part, PART, scatter_dimension=0, tiled=True)  49.9 us
    all_gather x1, waiting for transfers between devices, body(): both = lax.all_gather(both, PART, axis=0, tiled=True)  38.3 us
    psum x2, blocking collectives, body(): part, norm = lax.psum(lax.psum((part, norm), ('dp', 'sub')), 'blk')  16.9 us
    dot_general x2, matrix products, scores(): jnp.einsum('rd,kd->rk', rows, protos, preferred_element_type=jnp.float32)  12.2 us
    convert_element_type x1, other arithmetic, body(): ((pred / norm[:, None] - row[:, None] * code * col[None, :]) / SOFTMAX_TE...  7.43 us
    reduce_sum x3, other arithmetic, body(): part = jnp.sum(code * col[None, :], axis=1)  7.06 us
    reduce_sum x2, other arithmetic, body(): col = 1.0 / jnp.sum(code * row[:, None], axis=0)  6.15 us
  transfers between devices with their start and end apart: 2, of which 2 were waited for; matrix products, arithmetic and copies ran while one was open for 3% of the time, Pallas kernels for 0%

profile of v1, /device:TPU:0, one launch (start us, length us, event | category | flops | bytes accessed | tf_op | source)
XLA Modules:
  0.0 228.2 jit_solution(5296620620910135981)
XLA Ops:
  7.2 0.0 all-gather.2.cloned.1.call-start
  7.2 0.9 fusion.17
  8.1 0.9 fusion.19
  9.0 0.9 fusion.18
  9.9 0.6 pad_maximum_fusion
  10.5 0.0 all-gather.2.cloned.1.call-update
  10.5 0.0 reduce-scatter.2.cloned.1.call-start
  10.6 1.6 fusion.10
  12.2 0.9 convolution_compare_fusion
  13.1 38.3 %all-gather.2.cloned.1.call-done = bf16[1024,512]{1,0:T(8,128)(2,1)} async-done(((bf16[64,512]{1,0:T(8,128)(2,1)}), bf16[1024,512]{1,0:T(8,128)(2,1)}) %all-gather.2.cloned.1.call-update) | async-done | bytes 1048592 | tf_op jit(solution)/shard_map/all_gather | solution.py:31
  51.4 0.6 broadcast_in_dim.6
  52.0 0.0 copy-start.2
  52.0 4.4 %convert_reduce_fusion = (f32[2048]{0:T(1024)S(1)}, bf16[1024,2048]{1,0:T(8,128)(2,1)S(1)}) fusion(f32[2048]{0:T(1024)S(1)} %add_rsqrt_fusion, bf16[8192,256]{1,0:T(8,128)(2,1)} %param.7, s32[]{:T(128)S(6)} %select_n.14, bf16[1024,512]{1,0:T(8,128)(2,1)} %all-gather.2.cloned.1.call-done, pred[128,8,16,128]{3,2,1,0:T(8,128)(4,1)S(1)} %bitcast.11), kind=kOutput, calls=%fused_computation.6 | convolution fusion | flops 1087895552 | bytes 7880708 | tf_op jit(solution)/shard_map/rd,kd->rk/dot_general | solution.py:45
  56.4 0.0 copy-start
  56.5 0.9 fusion
  57.4 0.0 copy-done.2
  57.4 7.8 %fusion.9 = (f32[1024]{0:T(1024)S(1)}, f32[1024,2048]{1,0:T(8,128)}) fusion(pred[128,8,16,128]{3,2,1,0:T(8,128)(4,1)S(1)} %bitcast.12, f32[2048]{0:T(1024)S(1)} %add_rsqrt_fusion, bf16[8192,256]{1,0:T(8,128)(2,1)} %param.7, s32[]{:T(128)S(6)} %select_n.14, bf16[1024,512]{1,0:T(8,128)(2,1)S(1)} %copy-done.2), kind=kOutput, calls=%fused_computation.18 | convolution fusion | flops 1083702272 | bytes 12070916 | tf_op jit(solution)/shard_map/rd,kd->rk/dot_general | solution.py:45
  65.2 0.0 copy-done
  65.2 6.1 %all-reduce = (f32[1024]{0:T(1024)S(1)}, f32[1024]{0:T(1024)S(1)}) all-reduce(f32[1024]{0:T(1024)S(1)} %fusion, f32[1024]{0:T(1024)S(1)} %get-tuple-element.8), channel_id=1, replica_groups=mesh['groups'=2,'blk'=4,'dp'=2,'sub'=2] {'dp','sub'}, use_global_device_ids=true, to_apply=%region_8.9 | all-reduce | flops 2048 | bytes 16384 | tf_op jit(solution)/shard_map/psum | solution.py:58
  71.3 10.8 %all-reduce.1 = (f32[1024]{0:T(1024)S(1)}, f32[1024]{0:T(1024)S(1)}) all-reduce(f32[1024]{0:T(1024)S(1)} %get-tuple-element.2, f32[1024]{0:T(1024)S(1)} %get-tuple-element.3), channel_id=1, replica_groups=mesh['groups'=2,'blk'=4,'dp'=2,'sub'=2] {'blk'}, use_global_device_ids=true, to_apply=%region_9.10 | all-reduce | flops 2048 | bytes 16384 | tf_op jit(solution)/shard_map/psum | solution.py:58
  82.1 3.1 %fusion.1 = f32[2048]{0:T(1024)S(1)} fusion(bf16[1024,2048]{1,0:T(8,128)(2,1)} %copy-done, f32[1024]{0:T(1024)S(1)} %broadcast_divide_fusion.5), kind=kLoop, calls=%fused_computation.8 | loop fusion | flops 6289408 | bytes 4206592 | tf_op jit(solution)/shard_map/reduce_sum | solution.py:55
  85.2 3.1 %fusion.2 = f32[1024]{0:T(1024)S(1)} fusion(bf16[1024,2048]{1,0:T(8,128)(2,1)} %copy-done, f32[2048]{0:T(1024)S(1)} %broadcast_divide_fusion.1), kind=kLoop, calls=%fused_computation.9 | loop fusion | flops 6290432 | bytes 4206592 | tf_op jit(solution)/shard_map/reduce_sum | solution.py:56
  88.3 29.7 %psum.46 = f32[1024]{0:T(1024)S(1)} all-reduce(f32[1024]{0:T(1024)S(1)} %fusion.2), channel_id=1, replica_groups=mesh['groups'=2,'blk'=4,'dp'=2,'sub'=2] {'blk','dp','sub'}, use_global_device_ids=true, to_apply=%region_12.13 | all-reduce | flops 1024 | bytes 8192 | tf_op jit(solution)/shard_map/psum | solution.py:60
  118.0 3.1 %fusion.3 = f32[2048]{0:T(1024)S(1)} fusion(bf16[1024,2048]{1,0:T(8,128)(2,1)} %copy-done, f32[1024]{0:T(1024)S(1)} %broadcast_divide_fusion.4), kind=kLoop, calls=%fused_computation.10 | loop fusion | flops 6289408 | bytes 4206592 | tf_op jit(solution)/shard_map/reduce_sum | solution.py:55
  121.1 3.1 %fusion.4 = f32[1024]{0:T(1024)S(1)} fusion(bf16[1024,2048]{1,0:T(8,128)(2,1)} %copy-done, f32[2048]{0:T(1024)S(1)} %broadcast_divide_fusion), kind=kLoop, calls=%fused_computation.11 | loop fusion | flops 6290432 | bytes 4206592 | tf_op jit(solution)/shard_map/reduce_sum | solution.py:56
  124.1 29.5 %psum.47 = f32[1024]{0:T(1024)S(1)} all-reduce(f32[1024]{0:T(1024)S(1)} %fusion.4), channel_id=1, replica_groups=mesh['groups'=2,'blk'=4,'dp'=2,'sub'=2] {'blk','dp','sub'}, use_global_device_ids=true, to_apply=%region_15.16 | all-reduce | flops 1024 | bytes 8192 | tf_op jit(solution)/shard_map/psum | solution.py:60
  153.6 7.4 %fusion.8 = bf16[1024,2048]{1,0:T(8,128)(2,1)S(1)} fusion(bf16[1024,2048]{1,0:T(8,128)(2,1)} %copy-done, f32[1024,2048]{1,0:T(8,128)} %get-tuple-element.9, pred[128,8,16,128]{3,2,1,0:T(8,128)(4,1)S(1)} %bitcast.13, f32[1024]{0:T(1024)S(1)} %broadcast_divide_fusion.3, f32[2048]{0:T(1024)S(1)} %broadcast_divide_fusion, f32[1024]{0:T(1024)S(1)} %get-tuple-element.5), kind=kLoop, calls=%fused_computation.15 | loop fusion | flops 20971520 | bytes 18890752 | tf_op jit(solution)/shard_map/convert_element_type | solution.py:62
  161.1 0.0 copy-start.1
  161.1 1.9 copy-done.1
  163.0 3.6 %fusion.25 = f32[1024,256]{1,0:T(8,128)} fusion(bf16[1024,2048]{1,0:T(8,128)(2,1)S(1)} %fusion.8, f32[2048]{0:T(1024)S(1)} %add_rsqrt_fusion, bf16[8192,256]{1,0:T(8,128)(2,1)} %param.7, s32[]{:T(128)S(6)} %select_n.14), kind=kOutput, calls=%fused_computation.52 | convolution fusion | flops 1075314688 | bytes 6299652 | tf_op jit(solution)/shard_map/dot_general | solution.py:65
  166.6 0.0 reduce-scatter.2.cloned.1.call-update
  166.6 4.9 %fusion.13 = f32[2048,256]{1,0:T(8,128)} fusion(bf16[1024,2048]{1,0:T(8,128)(2,1)} %copy-done.1, bf16[1024,512]{1,0:T(8,128)(2,1)S(1)} %copy-done.2), kind=kOutput, calls=%fused_computation.25 | convolution fusion | flops 1073741824 | bytes 6815744 | tf_op jit(solution)/shard_map/rk,rd->kd/dot_general | solution.py:66
  171.5 49.9 %reduce-scatter.2.cloned.1.call-done = f32[64,256]{1,0:T(8,128)} async-done(((f32[1024,256]{1,0:T(8,128)}), f32[64,256]{1,0:T(8,128)}) %reduce-scatter.2.cloned.1.call-update) | async-done | bytes 65552 | tf_op jit(solution)/shard_map/reduce_scatter | solution.py:67
  (9 shorter events, 0.0 us)
Async XLA Ops:
  7.2 44.2 %all-gather.2.cloned.1.call-start = ((), (), s32[]{:S(2)}) async-start(), calls=%async_computation.1 | async-start | bytes 1114112 | tf_op jit(solution)/shard_map/all_gather | solution.py:31
  10.5 210.9 %reduce-scatter.2.cloned.1.call-start = ((), (), s32[]{:S(2)}) async-start(), calls=%async_computation.2 | async-start | bytes 1114112 | tf_op jit(solution)/shard_map/reduce_scatter | solution.py:67
  52.0 5.3 %copy-start.2 = (bf16[1024,512]{1,0:T(8,128)(2,1)S(1)}, bf16[1024,512]{1,0:T(8,128)(2,1)}, u32[]{:S(2)}) copy-start(bf16[1024,512]{1,0:T(8,128)(2,1)} %all-gather.2.cloned.1.call-done) | copy-start | bytes 3145732
  56.4 8.7 %copy-start = (bf16[1024,2048]{1,0:T(8,128)(2,1)}, bf16[1024,2048]{1,0:T(8,128)(2,1)S(1)}, u32[]{:S(2)}) copy-start(bf16[1024,2048]{1,0:T(8,128)(2,1)S(1)} %get-tuple-element.7) | copy-start | bytes 12582916
  161.1 1.9 copy-start.1
Sparse Core Ops, SparseCore 0:
  10.7 40.6 all-gather.1
  166.7 54.6 reduce-scatter.1
